TPU v7x, 256 devices: a whole 4x4x8 slice. The times are simulated.
256 devices in a mesh: row: 16 (over z, core), col: 16 (over x, y).
Axes of the slice: x: 4, y: 4, z: 8, core: 2. Of those that a mesh axis runs over, the one named last changes fastest.
Arguments:
- panel: float32 [16384, 128], P(('row', 'col')), as said below
- mobility: float32 [16384, 16384], P('row', 'col'), as said below
Outputs:
- updated: float32 [16384, 16384], P('row', 'col')
- panel_factor: float32 [128, 128], replicated
Inputs may be any that keep to these rules, and one draw needn't show every extreme that they name: Each row and each column of the panel has its own scale. `mobility`: Symmetric.
All inputs are finite; a program needn't handle non-finite values.
Results may differ from a plain program's by a relative error of at most 0.000076.
Values sent between devices are 32-bit elements; how exact they have to be, the bound alone decides.
No kernel may reach another device: no remote copies, remote signals or barrier semaphores. Data moves between devices by JAX's collectives and lax.ppermute only.
A program may use at most 64 MiB of HBM per device.

v0:
```python
import jax
import jax.numpy as jnp
from jax import lax
from jax.sharding import PartitionSpec as P


def spread(shard, axis, root):
    mine = lax.axis_index(axis) == root
    return lax.psum(jnp.where(mine, shard, jnp.zeros_like(shard)), axis)


def product(first_op, second_op):
    return jnp.dot(
        first_op, second_op, precision=lax.Precision.HIGHEST, preferred_element_type=jnp.float32
    )


def product_tn(first_op, second_op):
    return lax.dot_general(
        first_op,
        second_op,
        (((0,), (0,)), ((), ())),
        precision=lax.Precision.HIGHEST,
        preferred_element_type=jnp.float32,
    )


def product_nt(first_op, second_op):
    return lax.dot_general(
        first_op,
        second_op,
        (((1,), (1,)), ((), ())),
        precision=lax.Precision.HIGHEST,
        preferred_element_type=jnp.float32,
    )


def invert_core(core_matrix):
    identity = jnp.eye(core_matrix.shape[0], dtype=jnp.float32)

    def newton_step(index, approx):
        return product(approx, 2.0 * identity - product(core_matrix, approx))

    return lax.fori_loop(0, 12, newton_step, identity)


def correction_columns(block_rows_arr, block_ratio):
    root_index = lax.axis_index("col") * block_ratio + 0
    copies = spread(block_rows_arr, "row", root_index)
    return copies


def on_device(panel, mobility):
    piece_rows = panel.shape[0]
    width_cols = panel.shape[1]
    count_col = lax.axis_size("col")
    count_row = lax.axis_size("row")
    block_ratio = count_row // count_col
    row_index = lax.axis_index("row")
    col_index = lax.axis_index("col")
    block_rows = mobility.shape[0]
    block_cols = mobility.shape[1]
    first_row = (row_index * count_col + col_index) * piece_rows
    positions = first_row + jnp.arange(piece_rows, dtype=jnp.int32)
    selector = (jnp.arange(width_cols, dtype=jnp.int32)[:, None] == positions[None, :]).astype(
        jnp.float32
    )
    gram_term = product_tn(panel, panel)
    top_term = product(selector, panel)
    gram_sum, top_rows = lax.psum((gram_term, top_term), ("row", "col"))
    lower_factor = jnp.linalg.cholesky(gram_sum)
    panel_factor = lower_factor.T
    ortho_piece = jax.scipy.linalg.solve_triangular(lower_factor, panel.T, lower=True).T
    basis_piece = ortho_piece + selector.T
    top_ortho = jax.scipy.linalg.solve_triangular(lower_factor, top_rows.T, lower=True)
    core_matrix = jnp.eye(width_cols, dtype=jnp.float32) + top_ortho
    kernel = invert_core(core_matrix)
    everything = lax.all_gather(basis_piece, ("row", "col"), axis=0, tiled=True)
    basis_rows = lax.dynamic_slice_in_dim(everything, row_index * block_rows, block_rows, 0)
    basis_cols = lax.dynamic_slice_in_dim(everything, col_index * block_cols, block_cols, 0)
    partial_rows = product(mobility, basis_cols)
    spread_rows = product(lax.psum(partial_rows, "col"), kernel)
    inner_sum = lax.psum(product_tn(basis_rows, spread_rows), "row")
    inner = product_tn(kernel, inner_sum)
    correction_rows = spread_rows - 0.5 * product(basis_rows, inner)
    correction_cols = correction_columns(correction_rows, block_ratio)
    left_side = jnp.concatenate([basis_rows, correction_rows], axis=1)
    right_side = jnp.concatenate([correction_cols, basis_cols], axis=1)
    updated = mobility - product_nt(left_side, right_side)
    return (updated, panel_factor)


def solution(mesh):
    in_specs = (P(("row", "col"), None), P("row", "col"))
    out_specs = (P("row", "col"), P())
    return jax.shard_map(
        on_device, mesh=mesh, in_specs=in_specs, out_specs=out_specs, check_vma=False
    )
```

profile of v0, /device:TPU:1, one launch (start us, length us, event | category | flops | bytes accessed | tf_op | source)
XLA Modules:
  0.0 727.7 jit_solution(3753922273948830282)
XLA Ops:
  7.2 0.0 copy-start
  7.2 0.0 all-reduce.12.cloned.1.call-start
  7.2 0.7 copy-done
  7.9 0.9 fusion.18
  8.8 0.8 fusion.14
  9.6 0.0 all-reduce.12.cloned.1.call-update
  9.7 0.0 all-gather.2.cloned.1.call-start
  9.7 249.4 %all-reduce.12.cloned.1.call-done = (f32[128,128]{0,1:T(8,128)}, f32[128,128]{1,0:T(8,128)}) async-done(((f32[128,128]{0,1:T(8,128)}, f32[128,128]{1,0:T(8,128)}), (f32[128,128]{0,1:T(8,128)}, f32[128,128]{1,0:T(8,128)})) %all-reduce.12.cloned.1.call-update) | async-done | bytes 131088 | tf_op jit(solution)/shard_map/psum | solution.py:70
  259.1 0.9 copy.5
  260.0 0.9 fusion.12
  260.9 11.7 %cholesky.19 = f32[128,128]{1,0:T(8,128)S(1)} custom-call(f32[128,128]{1,0:T(8,128)S(1)} %fusion.12), custom_call_target="Cholesky" | custom-call | tf_op jit(solution)/shard_map/jit(cholesky)/cholesky | solution.py:71
  272.6 0.6 compare_reduce_fusion
  273.3 0.7 fusion.15
  273.9 9.8 %custom-call.10 = f32[1,128,128]{1,2,0:T(8,128)S(1)} custom-call(f32[1,128,128]{2,1,0:T(8,128)S(1)} %get-tuple-element.49), custom_call_target="InvertDiagBlocksLowerTriangular" | custom-call | tf_op jit(solution)/shard_map/jit(_solve_triangular)/triangular_solve | solution.py:73
  283.8 0.8 fusion.3
  284.6 0.0 all-gather.2.cloned.1.call-update
  284.6 0.0 all-reduce.6.cloned.1.call-start
  284.7 0.1 copy.6
  284.7 1.1 convolution_add_fusion
  285.9 115.3 %all-gather.2.cloned.1.call-done = f32[16384,128]{1,0:T(8,128)} async-done(((f32[64,128]{1,0:T(8,128)}), f32[16384,128]{1,0:T(8,128)}) %all-gather.2.cloned.1.call-update) | async-done | bytes 8388624 | tf_op jit(solution)/shard_map/all_gather | solution.py:78
  401.2 1.3 constant_dynamic-slice_fusion.1
  402.5 7.5 %convolution_bitcast_fusion.1 = f32[1024,128]{0,1:T(8,128)} fusion(f32[1024,128]{1,0:T(8,128)S(1)} %get-tuple-element.47, f32[1024,1024]{1,0:T(8,128)} %param.5), kind=kOutput, calls=%fused_computation.7 | convolution fusion | flops 1610612736 | bytes 5242880 | tf_op jit(solution)/shard_map/dot_general | solution.py:13
  409.9 0.0 all-reduce.6.cloned.1.call-update
  410.0 0.2 all-reduce.8.cloned.1.call-start
  410.2 7.1 while.11
  410.2 0.3 convolution_subtract_fusion.3
  410.5 0.3 convolution_bitcast_fusion.4
  410.8 0.3 convolution_subtract_fusion.3
  411.1 0.3 convolution_bitcast_fusion.4
  411.4 0.3 convolution_subtract_fusion.3
  411.7 0.3 convolution_bitcast_fusion.4
  412.0 0.3 convolution_subtract_fusion.3
  412.3 0.3 convolution_bitcast_fusion.4
  412.6 0.3 convolution_subtract_fusion.3
  412.9 0.3 convolution_bitcast_fusion.4
  413.2 0.3 convolution_subtract_fusion.3
  413.5 0.3 convolution_bitcast_fusion.4
  413.8 0.3 convolution_subtract_fusion.3
  414.0 0.3 convolution_bitcast_fusion.4
  414.4 0.3 convolution_subtract_fusion.3
  414.6 0.3 convolution_bitcast_fusion.4
  415.0 0.3 convolution_subtract_fusion.3
  415.2 0.3 convolution_bitcast_fusion.4
  415.6 0.3 convolution_subtract_fusion.3
  415.8 0.3 convolution_bitcast_fusion.4
  416.1 0.3 convolution_subtract_fusion.3
  416.4 0.3 convolution_bitcast_fusion.4
  416.7 0.3 convolution_subtract_fusion.3
  417.0 0.3 convolution_bitcast_fusion.4
  417.3 83.1 %all-reduce.6.cloned.1.call-done = f32[1024,128]{0,1:T(8,128)} async-done(((f32[1024,128]{0,1:T(8,128)}), f32[1024,128]{0,1:T(8,128)}) %all-reduce.6.cloned.1.call-update) | async-done | bytes 524304 | tf_op jit(solution)/shard_map/psum | solution.py:82
  500.4 1.6 fusion.19
  502.1 1.6 fusion.20
  503.7 0.0 all-reduce.8.cloned.1.call-update
  503.7 0.0 all-reduce.10.cloned.1.call-start
  503.8 0.2 copy.8
  504.0 99.9 %all-reduce.8.cloned.1.call-done = f32[128,128]{1,0:T(8,128)} async-done(((f32[128,128]{1,0:T(8,128)}), f32[128,128]{1,0:T(8,128)}) %all-reduce.8.cloned.1.call-update) | async-done | bytes 65552 | tf_op jit(solution)/shard_map/psum | solution.py:83
  603.9 1.0 fusion.21
  604.9 1.4 broadcast_select_fusion
  606.3 0.0 all-reduce.10.cloned.1.call-update
  606.3 0.7 copy.9
  607.1 107.4 %all-reduce.10.cloned.1.call-done = f32[1024,128]{1,0:T(8,128)} async-done(((f32[1024,128]{1,0:T(8,128)}), f32[1024,128]{1,0:T(8,128)}) %all-reduce.10.cloned.1.call-update) | async-done | bytes 524304 | tf_op jit(solution)/shard_map/psum | solution.py:9
  714.4 6.7 convolution_subtract_fusion.1
  (15 shorter events, 0.1 us)
Async XLA Ops:
  7.2 0.8 copy-start
  7.2 251.9 %all-reduce.12.cloned.1.call-start = ((), (), s32[]{:S(2)}) async-start(), calls=%async_computation.4 | async-start | bytes 262144 | tf_op jit(solution)/shard_map/psum | solution.py:70
  9.7 391.5 %all-gather.2.cloned.1.call-start = ((), (), s32[]{:S(2)}) async-start(), calls=%async_computation | async-start | bytes 8421376 | tf_op jit(solution)/shard_map/all_gather | solution.py:78
  284.6 215.8 %all-reduce.6.cloned.1.call-start = ((), (), s32[]{:S(2)}) async-start(), calls=%async_computation.1 | async-start | bytes 1048576 | tf_op jit(solution)/shard_map/psum | solution.py:82
  410.0 193.9 %all-reduce.8.cloned.1.call-start = ((), (), s32[]{:S(2)}) async-start(), calls=%async_computation.2 | async-start | bytes 131072 | tf_op jit(solution)/shard_map/psum | solution.py:83
  503.7 210.7 %all-reduce.10.cloned.1.call-start = ((), (), s32[]{:S(2)}) async-start(), calls=%async_computation.3 | async-start | bytes 1048576 | tf_op jit(solution)/shard_map/psum | solution.py:9
Sparse Core Ops, SparseCore 0:
  14.2 244.8 all-reduce.11
  284.7 116.4 all-gather.1
  410.1 90.2 all-reduce.5
  503.8 99.9 all-reduce.7
  606.6 107.7 all-reduce.9
where the time goes:
time: 728 us
  waiting for transfers between devices  655 us (90%)
  matrix products  30.2 us (4%)
  other arithmetic  23.7 us (3%)
  between operations  13.9 us (2%)
    psum x1, waiting for transfers between devices, on_device(): gram_sum, top_rows = lax.psum((gram_term, top_term), ('row', 'col'))  249 us
    all_gather x1, waiting for transfers between devices, on_device(): everything = lax.all_gather(basis_piece, ('row', 'col'), axis=0, tiled=True)  115 us
    psum x1, waiting for transfers between devices, spread(): return lax.psum(jnp.where(mine, shard, jnp.zeros_like(shard)), axis)  107 us
    psum x1, waiting for transfers between devices, on_device(): inner_sum = lax.psum(product_tn(basis_rows, spread_rows), 'row')  99.9 us
    psum x1, waiting for transfers between devices, on_device(): spread_rows = product(lax.psum(partial_rows, 'col'), kernel)  83.1 us
    dot_general x28, matrix products, product(): jnp.dot(first_op, second_op, precision=lax.Precision.HIGHEST, preferred_e...  17.9 us
  transfers between devices with their start and end apart: 5, of which 5 were waited for; matrix products, arithmetic and copies ran while one was open for 1% of the time, Pallas kernels for 0%

commit v1 on v0

--- a/solution.py
+++ b/solution.py
@@ -80,7 +80,7 @@
     basis_cols = lax.dynamic_slice_in_dim(everything, col_index * block_cols, block_cols, 0)
     partial_rows = product(mobility, basis_cols)
     spread_rows = product(lax.psum(partial_rows, "col"), kernel)
-    inner_sum = lax.psum(product_tn(basis_rows, spread_rows), "row")
+    inner_sum = jnp.sum(lax.all_gather(product_tn(basis_rows, spread_rows), "row"), axis=0)
     inner = product_tn(kernel, inner_sum)
     correction_rows = spread_rows - 0.5 * product(basis_rows, inner)
     correction_cols = correction_columns(correction_rows, block_ratio)

time: 728 us -> 668 us (0.918)
  waiting for transfers between devices: 655 us -> 595 us
    psum x1 -> x0, waiting for transfers between devices: 99.9 us -> none  [on_device(): inner_sum = lax.psum(product_tn(basis_rows, spread_rows), 'row')]
    all_gather x0 -> x1, waiting for transfers between devices: none -> 39.6 us  [on_device(): lax.all_gather(product_tn(basis_rows, spread_rows), 'row')]
where the time goes in v1:
time: 668 us
  waiting for transfers between devices  595 us (89%)
  matrix products  29.3 us (4%)
  other arithmetic  25 us (4%)
  between operations  13.9 us (2%)
    psum x1, waiting for transfers between devices, on_device(): gram_sum, top_rows = lax.psum((gram_term, top_term), ('row', 'col'))  249 us
    all_gather x1, waiting for transfers between devices, on_device(): everything = lax.all_gather(basis_piece, ('row', 'col'), axis=0, tiled=True)  115 us
    psum x1, waiting for transfers between devices, spread(): return lax.psum(jnp.where(mine, shard, jnp.zeros_like(shard)), axis)  107 us
    psum x1, waiting for transfers between devices, on_device(): spread_rows = product(lax.psum(partial_rows, 'col'), kernel)  83.1 us
    all_gather x1, waiting for transfers between devices, on_device(): lax.all_gather(product_tn(basis_rows, spread_rows), 'row')  39.6 us
    dot_general x28, matrix products, product(): jnp.dot(first_op, second_op, precision=lax.Precision.HIGHEST, preferred_e...  17.9 us
  transfers between devices with their start and end apart: 5, of which 5 were waited for; matrix products, arithmetic and copies ran while one was open for 1% of the time, Pallas kernels for 0%

profile of v1, /device:TPU:1, one launch (start us, length us, event | category | flops | bytes accessed | tf_op | source)
XLA Modules:
  0.0 667.6 jit_solution(783375300945159928)
XLA Ops:
  7.2 0.0 copy-start
  7.2 0.0 all-reduce.9.cloned.1.call-start
  7.2 0.7 copy-done
  7.9 0.9 fusion.18
  8.8 0.8 fusion.14
  9.6 0.0 all-reduce.9.cloned.1.call-update
  9.7 0.0 all-gather.4.cloned.1.call-start
  9.7 249.4 %all-reduce.9.cloned.1.call-done = (f32[128,128]{0,1:T(8,128)}, f32[128,128]{1,0:T(8,128)}) async-done(((f32[128,128]{0,1:T(8,128)}, f32[128,128]{1,0:T(8,128)}), (f32[128,128]{0,1:T(8,128)}, f32[128,128]{1,0:T(8,128)})) %all-reduce.9.cloned.1.call-update) | async-done | bytes 131088 | tf_op jit(solution)/shard_map/psum | solution.py:70
  259.1 0.9 copy.5
  260.0 0.9 fusion.12
  260.9 11.7 %cholesky.19 = f32[128,128]{1,0:T(8,128)S(1)} custom-call(f32[128,128]{1,0:T(8,128)S(1)} %fusion.12), custom_call_target="Cholesky" | custom-call | tf_op jit(solution)/shard_map/jit(cholesky)/cholesky | solution.py:71
  272.6 0.6 compare_reduce_fusion
  273.3 0.7 fusion.15
  273.9 9.8 %custom-call.10 = f32[1,128,128]{1,2,0:T(8,128)S(1)} custom-call(f32[1,128,128]{2,1,0:T(8,128)S(1)} %get-tuple-element.49), custom_call_target="InvertDiagBlocksLowerTriangular" | custom-call | tf_op jit(solution)/shard_map/jit(_solve_triangular)/triangular_solve | solution.py:73
  283.8 0.8 fusion.3
  284.6 0.0 all-gather.4.cloned.1.call-update
  284.6 0.0 all-reduce.5.cloned.1.call-start
  284.7 0.1 copy.6
  284.7 1.1 convolution_add_fusion
  285.9 115.3 %all-gather.4.cloned.1.call-done = f32[16384,128]{1,0:T(8,128)} async-done(((f32[64,128]{1,0:T(8,128)}), f32[16384,128]{1,0:T(8,128)}) %all-gather.4.cloned.1.call-update) | async-done | bytes 8388624 | tf_op jit(solution)/shard_map/all_gather | solution.py:78
  401.2 1.3 constant_dynamic-slice_fusion.1
  402.5 7.5 %convolution_bitcast_fusion.1 = f32[1024,128]{0,1:T(8,128)} fusion(f32[1024,128]{1,0:T(8,128)S(1)} %get-tuple-element.47, f32[1024,1024]{1,0:T(8,128)} %param.5), kind=kOutput, calls=%fused_computation.7 | convolution fusion | flops 1610612736 | bytes 5242880 | tf_op jit(solution)/shard_map/dot_general | solution.py:13
  409.9 0.0 all-reduce.5.cloned.1.call-update
  410.0 0.2 all-gather.6.cloned.1.call-start
  410.2 7.1 %while.11 = (s32[]{:T(128)}, f32[128,128]{0,1:T(8,128)S(1)}, f32[128,128]{1,0:T(8,128)S(1)}, s32[]{:T(128)}) while((s32[]{:T(128)}, f32[128,128]{0,1:T(8,128)S(1)}, f32[128,128]{1,0:T(8,128)S(1)}, s32[]{:T(128)}) %tuple.30), condition=%wide.region_6.7_spmd.clone, body=%wide.region_5.6_spmd.clone.sunk | while | flops 50380800 | bytes 524341 | solution.py:44
  410.2 0.3 convolution_subtract_fusion.3
  410.5 0.3 convolution_bitcast_fusion.4
  410.8 0.3 convolution_subtract_fusion.3
  411.1 0.3 convolution_bitcast_fusion.4
  411.4 0.3 convolution_subtract_fusion.3
  411.7 0.3 convolution_bitcast_fusion.4
  412.0 0.3 convolution_subtract_fusion.3
  412.3 0.3 convolution_bitcast_fusion.4
  412.6 0.3 convolution_subtract_fusion.3
  412.9 0.3 convolution_bitcast_fusion.4
  413.2 0.3 convolution_subtract_fusion.3
  413.5 0.3 convolution_bitcast_fusion.4
  413.8 0.3 convolution_subtract_fusion.3
  414.0 0.3 convolution_bitcast_fusion.4
  414.4 0.3 convolution_subtract_fusion.3
  414.6 0.3 convolution_bitcast_fusion.4
  415.0 0.3 convolution_subtract_fusion.3
  415.2 0.3 convolution_bitcast_fusion.4
  415.6 0.3 convolution_subtract_fusion.3
  415.8 0.3 convolution_bitcast_fusion.4
  416.1 0.3 convolution_subtract_fusion.3
  416.4 0.3 convolution_bitcast_fusion.4
  416.7 0.3 convolution_subtract_fusion.3
  417.0 0.3 convolution_bitcast_fusion.4
  417.3 83.1 %all-reduce.5.cloned.1.call-done = f32[1024,128]{0,1:T(8,128)} async-done(((f32[1024,128]{0,1:T(8,128)}), f32[1024,128]{0,1:T(8,128)}) %all-reduce.5.cloned.1.call-update) | async-done | bytes 524304 | tf_op jit(solution)/shard_map/psum | solution.py:82
  500.4 1.6 fusion.19
  502.1 1.6 fusion.20
  503.7 0.0 all-gather.6.cloned.1.call-update
  503.7 0.0 all-reduce.7.cloned.1.call-start
  503.8 0.2 copy.8
  504.0 39.6 %all-gather.6.cloned.1.call-done = f32[2048,128]{1,0:T(8,128)} async-done(((f32[128,128]{1,0:T(8,128)}), f32[2048,128]{1,0:T(8,128)}) %all-gather.6.cloned.1.call-update) | async-done | bytes 1048592 | tf_op jit(solution)/shard_map/all_gather | solution.py:83
  543.6 1.3 reduce_sum.9
  544.9 0.2 fusion.21
  545.1 1.4 broadcast_select_fusion
  546.5 0.0 all-reduce.7.cloned.1.call-update
  546.5 0.7 copy.9
  547.2 107.1 %all-reduce.7.cloned.1.call-done = f32[1024,128]{1,0:T(8,128)} async-done(((f32[1024,128]{1,0:T(8,128)}), f32[1024,128]{1,0:T(8,128)}) %all-reduce.7.cloned.1.call-update) | async-done | bytes 524304 | tf_op jit(solution)/shard_map/psum | solution.py:9
  654.3 6.8 %convolution_subtract_fusion.1 = f32[1024,1024]{1,0:T(8,128)} fusion(f32[1024,1024]{1,0:T(8,128)} %param.5, f32[1024,128]{1,0:T(8,128)S(1)} %get-tuple-element.51, f32[1024,128]{1,0:T(8,128)S(1)} %get-tuple-element.46, f32[1024,128]{1,0:T(8,128)S(1)} %get-tuple-element.47, f32[1024,128]{1,0:T(8,128)} %all-reduce.7.cloned.1.call-done), kind=kOutput, calls=%fused_computation.4 | convolution fusion | flops 3222798336 | bytes 10485760 | tf_op jit(solution)/shard_map/dot_general | solution.py:29
  (15 shorter events, 0.1 us)
Async XLA Ops:
  7.2 0.8 copy-start
  7.2 251.9 %all-reduce.9.cloned.1.call-start = ((), (), s32[]{:S(2)}) async-start(), calls=%async_computation.4 | async-start | bytes 262144 | tf_op jit(solution)/shard_map/psum | solution.py:70
  9.7 391.5 %all-gather.4.cloned.1.call-start = ((), (), s32[]{:S(2)}) async-start(), calls=%async_computation | async-start | bytes 8421376 | tf_op jit(solution)/shard_map/all_gather | solution.py:78
  284.6 215.8 %all-reduce.5.cloned.1.call-start = ((), (), s32[]{:S(2)}) async-start(), calls=%async_computation.1 | async-start | bytes 1048576 | tf_op jit(solution)/shard_map/psum | solution.py:82
  410.0 133.6 %all-gather.6.cloned.1.call-start = ((), (), s32[]{:S(2)}) async-start(), calls=%async_computation.3 | async-start | bytes 1114112 | tf_op jit(solution)/shard_map/all_gather | solution.py:83
  503.7 150.6 %all-reduce.7.cloned.1.call-start = ((), (), s32[]{:S(2)}) async-start(), calls=%async_computation.2 | async-start | bytes 1048576 | tf_op jit(solution)/shard_map/psum | solution.py:9
Sparse Core Ops, SparseCore 0:
  14.2 244.8 all-reduce.8
  284.7 116.4 all-gather.3
  410.1 90.2 all-reduce.4
  503.8 39.7 all-gather.5
  546.6 107.6 all-reduce.6
